TPU v7x, 128 devices: a whole 4x4x4 slice. The times are simulated.
128 devices in a mesh: seq: 16 (over z_lo, x, core), res: 8 (over y, z_hi).
Axes of the slice: x: 4, y: 4, z: 4 (z_hi: 2, z_lo: 2; z = z_hi * 2 + z_lo), core: 2. Of those that a mesh axis runs over, the one named last changes fastest.
Arguments:
- states: bfloat16 [512, 256, 768], P('seq', 'res'), may hold values from -6 to 6
- row_query: bfloat16 [768, 768], replicated, as said below
- row_key: bfloat16 [768, 768], replicated
- row_value: bfloat16 [768, 768], replicated, may hold values from -0.21875 to 0.21875
- row_out: bfloat16 [768, 768], replicated, may hold values from -0.21875 to 0.21875
- col_query: bfloat16 [768, 768], replicated, as said below
- col_key: bfloat16 [768, 768], replicated
- col_value: bfloat16 [768, 768], replicated, may hold values from -0.21875 to 0.21875
- col_out: bfloat16 [768, 768], replicated, may hold values from -0.21875 to 0.21875
Outputs:
- updated: bfloat16 [512, 256, 768], P('seq', 'res')
Inputs may be any that keep to these rules, and one draw needn't show every extreme that they name: No bound on the size of row_query and row_key entries or of the scores they give is promised. No bound on the size of col_query and col_key entries or of the scores they give is promised.
All inputs are finite; a program needn't handle non-finite values.
Results may differ from a plain program's by a relative error of at most 0.02.
Values may be sent and summed in bfloat16 or wider, within the bound.
A program may use at most 128 MiB of HBM per device.

v0:
```python
import math
import jax
import jax.numpy as jnp
from jax import lax
from jax.sharding import PartitionSpec as P

D = 768
HEADS = 12
HD = D // HEADS


def normalize(states):
    values = states.astype(jnp.float32)
    center = values - jnp.mean(values, axis=-1, keepdims=True)
    spread = jnp.mean(center * center, axis=-1, keepdims=True)
    return (center * lax.rsqrt(spread + 1e-05)).astype(jnp.bfloat16)


def project(inputs, weight):
    return jnp.dot(inputs, weight, preferred_element_type=jnp.float32)


def on_device(
    states, row_query, row_key, row_value, row_out, col_query, col_key, col_value, col_out
):
    rows, cols = (states.shape[0], states.shape[1])
    seq, res = (lax.axis_size("seq"), lax.axis_size("res"))
    own_rows, own_cols = (rows // res, cols // seq)
    all_rows, all_cols = (rows * seq, cols * res)
    tied_scale = HD ** (-0.5) / math.sqrt(all_rows)
    moved = lax.all_to_all(
        states.reshape(res, own_rows, cols, D), "res", split_axis=0, concat_axis=0
    )
    by_row = moved.transpose(1, 0, 2, 3).reshape(own_rows, all_cols, D)
    normed = normalize(by_row)
    q1 = project(normed, row_query).astype(jnp.bfloat16).reshape(own_rows, all_cols, HEADS, HD)
    k1 = project(normed, row_key).astype(jnp.bfloat16).reshape(own_rows, all_cols, HEADS, HD)
    v1 = project(normed, row_value).astype(jnp.bfloat16).reshape(own_rows, all_cols, HEADS, HD)
    part = jnp.einsum("rihd,rjhd->hij", q1, k1, preferred_element_type=jnp.float32) * tied_scale
    part = part.reshape(HEADS * all_cols, all_cols)
    tied = lax.psum_scatter(part, ("seq", "res"), scatter_dimension=0, tiled=True)
    prob1 = jax.nn.softmax(tied, axis=-1).astype(jnp.bfloat16)
    prob1 = lax.all_gather(prob1, ("seq", "res"), axis=0, tiled=True)
    prob1 = prob1.reshape(HEADS, all_cols, all_cols)
    o1 = jnp.einsum("hij,rjhd->rihd", prob1, v1, preferred_element_type=jnp.float32)
    o1 = o1.astype(jnp.bfloat16).reshape(own_rows, all_cols, D)
    mid = (by_row.astype(jnp.float32) + project(o1, row_out)).astype(jnp.bfloat16)
    mid = mid.reshape(own_rows, res, seq, own_cols, D).transpose(2, 1, 0, 3, 4)
    mid = mid.reshape(seq * res, own_rows, own_cols, D)
    mid = lax.all_to_all(mid, ("seq", "res"), split_axis=0, concat_axis=0)
    mid = mid.reshape(all_rows, own_cols, D).transpose(1, 0, 2)
    normed2 = normalize(mid)
    q2 = project(normed2, col_query).astype(jnp.bfloat16).reshape(own_cols, all_rows, HEADS, HD)
    k2 = project(normed2, col_key).astype(jnp.bfloat16).reshape(own_cols, all_rows, HEADS, HD)
    v2 = project(normed2, col_value).astype(jnp.bfloat16).reshape(own_cols, all_rows, HEADS, HD)
    score = jnp.einsum("crhd,cshd->chrs", q2, k2, preferred_element_type=jnp.float32)
    prob2 = jax.nn.softmax(score * HD ** (-0.5), axis=-1).astype(jnp.bfloat16)
    o2 = jnp.einsum("chrs,cshd->crhd", prob2, v2, preferred_element_type=jnp.float32)
    o2 = o2.astype(jnp.bfloat16).reshape(own_cols, all_rows, D)
    colupd = project(o2, col_out).astype(jnp.bfloat16)
    updated = (mid.astype(jnp.float32) + colupd.astype(jnp.float32)).astype(jnp.bfloat16)
    updated = updated.reshape(own_cols, seq, rows, D).transpose(1, 2, 0, 3)
    updated = lax.all_to_all(updated, "seq", split_axis=0, concat_axis=0)
    return updated.transpose(1, 0, 2, 3).reshape(rows, cols, D)


def solution(mesh):
    placed = (P("seq", "res", None), P(), P(), P(), P(), P(), P(), P(), P())
    return jax.shard_map(
        on_device, mesh=mesh, in_specs=placed, out_specs=P("seq", "res", None), check_vma=False
    )
```

profile of v0, /device:TPU:1, one launch (start us, length us, event | category | flops | bytes accessed | tf_op | source)
XLA Modules:
  0.0 1114.7 jit_solution(17327529294043333661)
XLA Ops:
  6.5 29.4 %all_to_all.15 = bf16[8,4,32,768]{3,2,1,0:T(8,128)(2,1)S(1)} all-to-all(bf16[8,4,32,768]{3,2,1,0:T(8,128)(2,1)} %bitcast.110), channel_id=1, replica_groups=mesh['seq'=16,'res'=8] {'res'}, dimensions={0} | all-to-all | bytes 3145728 | tf_op jit(solution)/shard_map/all_to_all | solution.py:31
  35.9 0.3 fusion.13
  36.2 0.1 div.31
  36.3 0.6 multiply_reduce_fusion.2
  37.0 0.4 convert_bitcast_fusion
  37.4 0.3 copy.94
  37.7 0.4 fusion.10
  38.1 1.3 copy-done.2
  39.4 1.1 copy-done.4
  40.5 1.4 convolution_convert_fusion.5
  41.9 0.7 copy.100
  42.6 4.3 convolution_convert_fusion.6
  46.9 1.7 copy.99
  48.6 2.3 bitcast_multiply_fusion
  51.0 0.2 all-gather.2.cloned.1.call-start
  51.2 633.3 %reduce-scatter.2.cloned.1.call-done = f32[24,256]{1,0:T(8,128)} async-done(((f32[3072,256]{1,0:T(8,128)}), f32[24,256]{1,0:T(8,128)}) %reduce-scatter.2.cloned.1.call-update) | async-done | bytes 24592 | tf_op jit(solution)/shard_map/reduce_scatter | solution.py:41
  684.5 0.8 reduce_max.18
  685.4 0.9 fusion.26
  686.3 1.4 divide_convert_fusion.4
  687.8 2.7 convolution_convert_fusion.7
  690.4 0.7 copy.98
  691.1 299.8 %all-gather.2.cloned.1.call-done = bf16[3072,256]{1,0:T(8,128)(2,1)} async-done(((bf16[24,256]{1,0:T(8,128)(2,1)}), bf16[3072,256]{1,0:T(8,128)(2,1)}) %all-gather.2.cloned.1.call-update) | async-done | bytes 1572880 | tf_op jit(solution)/shard_map/all_gather | solution.py:43
  990.9 2.1 fusion.15
  993.1 0.2 copy.102
  993.2 1.7 copy-done.3
  994.9 1.5 fusion.11
  996.5 0.6 reshape.103
  997.1 0.9 copy.138
  998.0 1.6 copy.105
  999.6 31.3 %all_to_all.16 = bf16[128,4,2,768]{3,2,1,0:T(2,128)(2,1)S(1)} all-to-all(bf16[128,4,2,768]{3,2,1,0:T(2,128)(2,1)S(1)} %copy.105), channel_id=1, replica_groups=mesh['seq'=16,'res'=8] {'seq','res'}, dimensions={0} | all-to-all | bytes 3145728 | tf_op jit(solution)/shard_map/all_to_all | solution.py:50
  1030.9 0.3 copy_convert_fusion
  1031.2 2.4 copy.107
  1033.6 0.3 bitcast_reduce_fusion
  1033.9 0.5 multiply_reduce_fusion.1
  1034.4 0.4 multiply_convert_fusion
  1034.8 1.1 copy-done.6
  1035.9 2.6 convolution_convert_fusion.1
  1038.5 2.6 copy.111
  1041.1 4.4 convolution_convert_fusion.2
  1045.5 2.5 convolution_convert_fusion.3
  1048.1 2.6 copy.109
  1050.7 2.6 copy.110
  1053.3 14.2 %fusion.30 = (f32[2,12,512]{2,1,0:T(8,128)S(1)}, f32[2,12,512,512]{2,3,1,0:T(8,128)}) fusion(bf16[2,512,12,64]{1,3,2,0:T(8,128)(2,1)} %bitcast.113, bf16[2,512,12,64]{1,3,2,0:T(8,128)(2,1)} %bitcast.111), kind=kOutput, calls=%fused_computation.55 | convolution fusion | flops 824181248 | bytes 28360704 | tf_op jit(solution)/shard_map/sub | solution.py:57
  1067.5 11.0 fusion.12
  1078.5 1.4 fusion.8
  1079.9 0.1 copy.137
  1080.1 25.8 %all_to_all.17 = bf16[16,32,2,768]{3,1,2,0:T(8,128)(2,1)S(1)} all-to-all(bf16[16,32,2,768]{3,1,2,0:T(8,128)(2,1)S(1)} %bitcast.105), channel_id=1, replica_groups=mesh['seq'=16,'res'=8] {'seq'}, dimensions={0} | all-to-all | bytes 3145728 | tf_op jit(solution)/shard_map/all_to_all | solution.py:63
  1105.9 2.0 copy.115
  (29 shorter events, 0.2 us)
Async XLA Ops:
  6.5 34.0 %copy-start = (bf16[768,768]{1,0:T(8,128)(2,1)S(1)}, bf16[768,768]{1,0:T(8,128)(2,1)}, u32[]{:S(2)}) copy-start(bf16[768,768]{1,0:T(8,128)(2,1)} %param.11) | copy-start | bytes 3538948
  6.5 678.0 %reduce-scatter.2.cloned.1.call-start = ((), (), s32[]{:S(2)}) async-start(), calls=%async_computation.4 | async-start | bytes 3170304 | tf_op jit(solution)/shard_map/reduce_scatter | solution.py:41
  37.7 1.7 copy-start.2
  39.4 1.1 copy-start.4
  50.9 636.8 %copy-start.5 = (bf16[4,256,768]{2,1,0:T(8,128)(2,1)S(1)}, bf16[4,256,768]{2,1,0:T(8,128)(2,1)}, u32[]{:S(2)}) copy-start(bf16[4,256,768]{2,1,0:T(8,128)(2,1)} %copy-done.4) | copy-start | bytes 4718596
  51.0 940.0 %all-gather.2.cloned.1.call-start = ((), (), s32[]{:S(2)}) async-start(), calls=%async_computation.5 | async-start | bytes 1585152 | tf_op jit(solution)/shard_map/all_gather | solution.py:43
  990.9 2.3 copy-start.8
  993.0 1.9 copy-start.3
  1034.4 1.5 copy-start.9
  1034.7 1.1 copy-start.6
  1041.1 4.4 copy-start.7
  1041.1 4.4 copy-start.10
  1067.5 11.0 copy-start.11
  1105.9 2.0 copy-start.1
Sparse Core Ops, SparseCore 0:
  51.1 633.3 reduce-scatter.1
  687.9 303.0 all-gather.1
where the time goes:
time: 1120 us; the launch traced here: 1110 us
  waiting for transfers between devices  933 us (83%)
  blocking collectives  86.4 us (8%)
  matrix products  50.5 us (5%)
  local copies, waits for them, and re-layouts  24.6 us (2%)
  between operations  13.6 us (1%)
    reduce_scatter x1, waiting for transfers between devices, on_device(): lax.psum_scatter(part, ('seq', 'res'), scatter_dimension=0, tiled=True)  633 us
    all_gather x1, waiting for transfers between devices, on_device(): prob1 = lax.all_gather(prob1, ('seq', 'res'), axis=0, tiled=True)  300 us
    all_to_all x1, blocking collectives, on_device(): mid = lax.all_to_all(mid, ('seq', 'res'), split_axis=0, concat_axis=0)  31.3 us
    all_to_all x1, blocking collectives, on_device(): lax.all_to_all(states.reshape(res, own_rows, cols, D), 'res', split_axis=...  29.4 us
    all_to_all x1, blocking collectives, on_device(): updated = lax.all_to_all(updated, 'seq', split_axis=0, concat_axis=0)  25.8 us
  transfers between devices with their start and end apart: 2, of which 2 were waited for; matrix products, arithmetic and copies ran while one was open for 0% of the time, Pallas kernels for 0%

commit v1 on v0

--- a/solution.py
+++ b/solution.py
@@ -7,6 +7,11 @@
 D = 768
 HEADS = 12
 HD = D // HEADS
+
+
+def all_by_exchange(shard, name, d):
+    sent = jnp.stack([shard] * lax.axis_size(name))
+    return jnp.concatenate(lax.all_to_all(sent, name, 0, 0), axis=d)
 
 
 def normalize(states):
@@ -40,7 +45,7 @@
     part = part.reshape(HEADS * all_cols, all_cols)
     tied = lax.psum_scatter(part, ("seq", "res"), scatter_dimension=0, tiled=True)
     prob1 = jax.nn.softmax(tied, axis=-1).astype(jnp.bfloat16)
-    prob1 = lax.all_gather(prob1, ("seq", "res"), axis=0, tiled=True)
+    prob1 = all_by_exchange(prob1, ("seq", "res"), 0)
     prob1 = prob1.reshape(HEADS, all_cols, all_cols)
     o1 = jnp.einsum("hij,rjhd->rihd", prob1, v1, preferred_element_type=jnp.float32)
     o1 = o1.astype(jnp.bfloat16).reshape(own_rows, all_cols, D)

time: 1120 us -> 846 us (0.76)
  waiting for transfers between devices: 933 us -> 652 us
  starting transfers between devices: 0.22 us -> 13.8 us
    all_gather x1 -> x0, waiting for transfers between devices: 300 us -> none  [on_device(): prob1 = lax.all_gather(prob1, ('seq', 'res'), axis=0, tiled=True)]
    all_to_all x0 -> x1, waiting for transfers between devices: none -> 18 us  [all_by_exchange(): return jnp.concatenate(lax.all_to_all(sent, name, 0, 0), axis=d)]
    all_to_all x0 -> x1, starting transfers between devices: none -> 13.8 us  [all_by_exchange(): return jnp.concatenate(lax.all_to_all(sent, name, 0, 0), axis=d)]
  transfers between devices with their start and end apart: 2 -> 2, of which waited for: 2 -> 2; matrix products, arithmetic and copies ran while one was open for 0% -> 1% of each run, Pallas kernels for 0% -> 0%
where the time goes in v1:
time: 846 us
  waiting for transfers between devices  652 us (77%)
  blocking collectives  83.9 us (10%)
  matrix products  50.1 us (6%)
  local copies, waits for them, and re-layouts  26.9 us (3%)
  starting transfers between devices  13.8 us (2%)
  between operations  13.6 us (2%)
    reduce_scatter x1, waiting for transfers between devices, on_device(): lax.psum_scatter(part, ('seq', 'res'), scatter_dimension=0, tiled=True)  634 us
    all_to_all x1, blocking collectives, on_device(): lax.all_to_all(states.reshape(res, own_rows, cols, D), 'res', split_axis=...  29.4 us
    all_to_all x1, blocking collectives, on_device(): mid = lax.all_to_all(mid, ('seq', 'res'), split_axis=0, concat_axis=0)  28.7 us
    all_to_all x1, blocking collectives, on_device(): updated = lax.all_to_all(updated, 'seq', split_axis=0, concat_axis=0)  25.8 us
    dot_general x8, matrix products, project(): return jnp.dot(inputs, weight, preferred_element_type=jnp.float32)  22 us
    all_to_all x1, waiting for transfers between devices, all_by_exchange(): return jnp.concatenate(lax.all_to_all(sent, name, 0, 0), axis=d)  18 us
  transfers between devices with their start and end apart: 2, of which 2 were waited for; matrix products, arithmetic and copies ran while one was open for 1% of the time, Pallas kernels for 0%

profile of v1, /device:TPU:1, one launch (start us, length us, event | category | flops | bytes accessed | tf_op | source)
XLA Modules:
  0.0 845.6 jit_solution(3438349429834159391)
XLA Ops:
  6.5 29.4 %all_to_all.20 = bf16[8,4,32,768]{3,2,1,0:T(8,128)(2,1)S(1)} all-to-all(bf16[8,4,32,768]{3,2,1,0:T(8,128)(2,1)} %bitcast.111), channel_id=1, replica_groups=mesh['seq'=16,'res'=8] {'res'}, dimensions={0} | all-to-all | bytes 3145728 | tf_op jit(solution)/shard_map/all_to_all | solution.py:36
  35.9 0.3 fusion.13
  36.3 0.6 multiply_reduce_fusion.2
  37.0 0.4 convert_bitcast_fusion
  37.4 0.3 copy.94
  37.7 0.4 fusion.10
  38.1 1.3 copy-done.2
  39.4 1.1 copy-done.4
  40.5 1.4 convolution_convert_fusion.5
  41.9 0.7 copy.100
  42.6 4.3 convolution_convert_fusion.6
  46.9 1.7 copy.99
  48.6 2.3 bitcast_multiply_fusion
  51.0 633.6 %reduce-scatter.2.cloned.1.call-done = f32[24,256]{1,0:T(8,128)} async-done(((f32[3072,256]{1,0:T(8,128)}), f32[24,256]{1,0:T(8,128)}) %reduce-scatter.2.cloned.1.call-update) | async-done | bytes 24592 | tf_op jit(solution)/shard_map/reduce_scatter | solution.py:46
  684.5 0.8 reduce_max.18
  685.4 0.9 fusion.26
  686.3 0.8 divide_convert_fusion.4
  687.1 1.2 stack.2
  688.4 13.8 %all-to-all-start.1 = ((bf16[128,24,256]{2,1,0:T(8,128)(2,1)}), bf16[128,24,256]{2,1,0:T(8,128)(2,1)S(1)}, u32[]{:S(2)}, u32[]{:S(2)}) async-start(bf16[128,24,256]{2,1,0:T(8,128)(2,1)} %stack.2), calls=%async_computation.2 | async-start | bytes 3145728 | tf_op jit(solution)/shard_map/all_to_all | solution.py:14
  702.2 3.8 convolution_convert_fusion.7
  706.0 1.7 copy.98
  707.8 18.0 %all-to-all-done.1 = bf16[128,24,256]{2,1,0:T(8,128)(2,1)S(1)} async-done(((bf16[128,24,256]{2,1,0:T(8,128)(2,1)}), bf16[128,24,256]{2,1,0:T(8,128)(2,1)S(1)}, u32[]{:S(2)}, u32[]{:S(2)}) %all-to-all-start.1) | async-done | bytes 1572896 | tf_op jit(solution)/shard_map/all_to_all | solution.py:14
  725.7 0.6 fusion.15
  726.3 0.2 copy.102
  726.5 0.5 copy-done.8
  727.0 1.3 copy-done.3
  728.3 1.5 fusion.11
  729.8 0.6 reshape.101
  730.5 0.9 copy.138
  731.3 1.6 copy.105
  733.0 28.7 %all_to_all.21 = bf16[128,4,2,768]{3,2,1,0:T(2,128)(2,1)S(1)} all-to-all(bf16[128,4,2,768]{3,2,1,0:T(2,128)(2,1)S(1)} %copy.105), channel_id=1, replica_groups=mesh['seq'=16,'res'=8] {'seq','res'}, dimensions={0} | all-to-all | bytes 3145728 | tf_op jit(solution)/shard_map/all_to_all | solution.py:55
  761.7 0.3 copy_convert_fusion
  762.0 2.4 copy.107
  764.4 0.3 bitcast_reduce_fusion
  764.7 0.5 multiply_reduce_fusion.1
  765.2 0.4 multiply_convert_fusion
  765.6 1.1 copy-done.6
  766.7 2.6 convolution_convert_fusion.1
  769.3 2.6 copy.111
  771.9 4.4 convolution_convert_fusion.2
  776.4 2.5 convolution_convert_fusion.3
  778.9 2.6 copy.109
  781.5 2.6 copy.110
  784.1 14.2 %fusion.30 = (f32[2,12,512]{2,1,0:T(8,128)S(1)}, f32[2,12,512,512]{2,3,1,0:T(8,128)}) fusion(bf16[2,512,12,64]{1,3,2,0:T(8,128)(2,1)} %bitcast.114, bf16[2,512,12,64]{1,3,2,0:T(8,128)(2,1)} %bitcast.112), kind=kOutput, calls=%fused_computation.55 | convolution fusion | flops 824181248 | bytes 28360704 | tf_op jit(solution)/shard_map/sub | solution.py:62
  798.3 11.0 %fusion.12 = bf16[2,12,64,512]{3,2,1,0:T(8,128)(2,1)S(1)} fusion(bf16[2,512,12,64]{1,3,2,0:T(8,128)(2,1)} %bitcast.113, f32[2,12,512,512]{2,3,1,0:T(8,128)} %get-tuple-element.6, f32[2,12,512]{2,1,0:T(8,128)S(1)} %get-tuple-element.5), kind=kOutput, calls=%fused_computation.22 | convolution fusion | flops 818675712 | bytes 28360704 | tf_op jit(solution)/shard_map/chrs,cshd->crhd/dot_general | solution.py:63
  809.3 1.4 fusion.8
  810.9 25.8 %all_to_all.22 = bf16[16,32,2,768]{3,1,2,0:T(8,128)(2,1)S(1)} all-to-all(bf16[16,32,2,768]{3,1,2,0:T(8,128)(2,1)S(1)} %bitcast.105), channel_id=1, replica_groups=mesh['seq'=16,'res'=8] {'seq'}, dimensions={0} | all-to-all | bytes 3145728 | tf_op jit(solution)/shard_map/all_to_all | solution.py:68
  836.7 2.0 copy.115
  (29 shorter events, 0.4 us)
Async XLA Ops:
  6.5 34.0 %copy-start = (bf16[768,768]{1,0:T(8,128)(2,1)S(1)}, bf16[768,768]{1,0:T(8,128)(2,1)}, u32[]{:S(2)}) copy-start(bf16[768,768]{1,0:T(8,128)(2,1)} %param.11) | copy-start | bytes 3538948
  6.5 678.0 %reduce-scatter.2.cloned.1.call-start = ((), (), s32[]{:S(2)}) async-start(), calls=%async_computation.5 | async-start | bytes 3170304 | tf_op jit(solution)/shard_map/reduce_scatter | solution.py:46
  37.7 1.7 copy-start.2
  39.4 1.1 copy-start.4
  688.4 13.9 %copy-start.5 = (bf16[4,256,768]{2,1,0:T(8,128)(2,1)S(1)}, bf16[4,256,768]{2,1,0:T(8,128)(2,1)}, u32[]{:S(2)}) copy-start(bf16[4,256,768]{2,1,0:T(8,128)(2,1)} %copy-done.4) | copy-start | bytes 4718596
  688.4 37.3 %all-to-all-start.1 = ((bf16[128,24,256]{2,1,0:T(8,128)(2,1)}), bf16[128,24,256]{2,1,0:T(8,128)(2,1)S(1)}, u32[]{:S(2)}, u32[]{:S(2)}) async-start(bf16[128,24,256]{2,1,0:T(8,128)(2,1)} %stack.2), calls=%async_computation.2 | async-start | bytes 3145728 | tf_op jit(solution)/shard_map/all_to_all | solution.py:14
  725.7 1.3 copy-start.8
  726.3 2.0 copy-start.3
  765.2 1.5 copy-start.9
  765.6 1.1 copy-start.6
  771.9 4.4 copy-start.7
  771.9 4.4 copy-start.10
  798.3 11.0 %copy-start.11 = (bf16[768,768]{1,0:T(8,128)(2,1)S(1)}, bf16[768,768]{1,0:T(8,128)(2,1)}, u32[]{:S(2)}) copy-start(bf16[768,768]{1,0:T(8,128)(2,1)} %param.17) | copy-start | bytes 3538948
  836.7 2.0 copy-start.1
Sparse Core Ops, SparseCore 0:
  51.1 633.3 reduce-scatter.1
